TPU v7x, 256 devices: a whole 4x4x8 slice. The times are simulated.
256 devices in a mesh: freq: 4 (over x_lo, core), rcv: 64 (over y, x_hi, z).
Axes of the slice: x: 4 (x_hi: 2, x_lo: 2; x = x_hi * 2 + x_lo), y: 4, z: 8, core: 2. Of those that a mesh axis runs over, the one named last changes fastest.
Arguments:
- spectra: bfloat16 [2, 128, 384, 8192], P(None, None, 'freq', 'rcv'), may hold values from -600 to 600
- valid: int32 [384, 8192], P(None, 'rcv'), may hold values from 0 to 1, as said below
- sources: int32 [256], P('rcv'), may hold values from 0 to 8191, as said below
- bounds: int32 [256, 8192, 2], P('freq', 'rcv'), may hold values from 0 to 128, as said below
Outputs:
- lag_corr: bfloat16 [256, 8192, 128], P('freq', 'rcv')
- peak_value: float32 [256, 8192], P('freq', 'rcv')
Inputs may be any that keep to these rules, and one draw needn't show every extreme that they name: `valid`: in each aligned group of 4 sub-windows at most one entry of a channel is 0. Source s is a channel from (s // 4) * 128 to (s // 4 + 1) * 128 - 1; the sources are distinct. bounds[s, c, 0] < bounds[s, c, 1] <= 128, and the window holds 16 to 64 lag samples.
All inputs are finite; a program needn't handle non-finite values.
Results may differ from a plain program's by a relative error of at most 0.007.
Values may be sent and summed in bfloat16 or wider, within the bound.
No kernel may reach another device: no remote copies, remote signals or barrier semaphores. Data moves between devices by JAX's collectives and lax.ppermute only.
A program may use at most 128 MiB of HBM per device.

v0:
```python
import math
import jax
import jax.numpy as jnp
from jax import lax
from jax.sharding import PartitionSpec as P

L = 128


def make_tables(bin_first, bin_count, lag_count, period):
    bins_col = (bin_first + 1 + jnp.arange(bin_count, dtype=jnp.int32))[:, None]
    lag_row = jnp.arange(lag_count, dtype=jnp.int32)[None, :] - lag_count // 2
    phase_int = bins_col * lag_row % period
    angles = phase_int.astype(jnp.float32) * (2.0 * math.pi / period)
    return (jnp.cos(angles).astype(jnp.bfloat16), jnp.sin(angles).astype(jnp.bfloat16))


def local(spectra, valid, sources, bounds):
    freq_index = lax.axis_index("freq")
    rcv_index = lax.axis_index("rcv")
    freq_count = lax.axis_size("freq")
    window_rows = spectra.shape[2]
    channels = valid.shape[1]
    own_valid = lax.dynamic_slice_in_dim(valid, freq_index * window_rows, window_rows, 0).astype(
        jnp.float32
    )
    spectra_f = spectra.astype(jnp.float32)
    energy = jnp.mean(spectra_f[0] * spectra_f[0] + spectra_f[1] * spectra_f[1], axis=0)
    scaling = own_valid / jnp.sqrt(energy + 1e-06)
    whitened = (spectra_f * scaling).astype(jnp.bfloat16)
    regrouped = lax.all_to_all(whitened, "freq", split_axis=1, concat_axis=2, tiled=True)
    bins_dev = regrouped.shape[1]
    offsets = sources - rcv_index * channels
    picked = jnp.take(regrouped, offsets, axis=3)
    valid_half = valid.astype(jnp.bfloat16)
    picked_valid = jnp.take(valid_half, offsets, axis=1)[None, None]
    source_part = lax.all_gather(picked, "rcv", axis=3, tiled=True)
    source_valid = lax.all_gather(picked_valid, "rcv", axis=3, tiled=True)
    part_re = jnp.einsum(
        "fws,fwc->fsc", source_part[0], regrouped[0], preferred_element_type=jnp.float32
    )
    part_re = part_re + jnp.einsum(
        "fws,fwc->fsc", source_part[1], regrouped[1], preferred_element_type=jnp.float32
    )
    part_im = jnp.einsum(
        "fws,fwc->fsc", source_part[0], regrouped[1], preferred_element_type=jnp.float32
    )
    part_im = part_im - jnp.einsum(
        "fws,fwc->fsc", source_part[1], regrouped[0], preferred_element_type=jnp.float32
    )
    counts_part = jnp.einsum(
        "wn,wc->nc", source_valid[0, 0], valid_half, preferred_element_type=jnp.float32
    )
    stack_re = (part_re / counts_part).astype(jnp.bfloat16)
    stack_im = (part_im / counts_part).astype(jnp.bfloat16)
    period = 2 * bins_dev * freq_count
    whole_re, whole_im = (
        lax.all_to_all(stack_re, "freq", split_axis=1, concat_axis=0, tiled=True),
        lax.all_to_all(stack_im, "freq", split_axis=1, concat_axis=0, tiled=True),
    )
    full_cos, full_sin = make_tables(0, bins_dev * freq_count, L, period)
    corr_sum = jnp.einsum(
        "fsc,ft->sct", whole_re, full_cos, preferred_element_type=jnp.float32
    ) - jnp.einsum("fsc,ft->sct", whole_im, full_sin, preferred_element_type=jnp.float32)
    lag_corr = corr_sum.astype(jnp.bfloat16)
    lag_index = jnp.arange(L, dtype=jnp.int32)[None, None, :]
    inside = (lag_index >= bounds[:, :, 0:1]) & (lag_index < bounds[:, :, 1:2])
    peak_value = jnp.max(jnp.where(inside, lag_corr.astype(jnp.float32), -jnp.inf), axis=2)
    return (lag_corr, peak_value)


def solution(mesh):
    in_specs = (P(None, None, "freq", "rcv"), P(None, "rcv"), P("rcv"), P("freq", "rcv", None))
    out_specs = (P("freq", "rcv", None), P("freq", "rcv"))
    return jax.shard_map(local, mesh=mesh, in_specs=in_specs, out_specs=out_specs, check_vma=False)
```

profile of v0, /device:TPU:1, one launch (start us, length us, event | category | flops | bytes accessed | tf_op | source)
XLA Modules:
  0.0 409.4 jit_solution(12215775478795225761)
XLA Ops:
  7.2 4.6 %copy_convert_fusion = f32[2,128,96,128]{3,2,0,1:T(8,128)S(1)} fusion(bf16[2,128,96,128]{3,2,1,0:T(8,128)(2,1)} %param.4), kind=kLoop, calls=%fused_computation.9 | loop fusion | flops 3145728 | bytes 18874368 | tf_op jit(solution)/shard_map/convert_element_type | solution.py:27
  11.7 0.0 copy-start.6
  11.7 0.9 fusion.1
  12.7 0.0 copy-done.6
  12.7 7.2 %multiply_convert_fusion = bf16[2,128,96,128]{3,2,0,1:T(8,128)(2,1)} fusion(f32[96,128]{1,0:T(8,128)S(1)} %rsqrt_multiply_fusion, bf16[2,128,96,128]{3,2,1,0:T(8,128)(2,1)} %param.4), kind=kLoop, calls=%fused_computation.2 | loop fusion | flops 9437184 | bytes 12632064 | tf_op jit(solution)/shard_map/convert_element_type | solution.py:30
  20.0 0.0 copy-start.8
  20.0 8.6 %all-to-all-start = ((bf16[2,128,96,128]{3,2,0,1:T(8,128)(2,1)}), bf16[2,128,96,128]{3,2,0,1:T(8,128)(2,1)}, u32[]{:S(2)}, u32[]{:S(2)}) async-start(bf16[2,128,96,128]{3,2,0,1:T(8,128)(2,1)} %multiply_convert_fusion), calls=%async_computation | async-start | bytes 12582912 | tf_op jit(solution)/shard_map/all_to_all | solution.py:31
  28.6 0.0 all-gather.2.cloned.1.call-start
  28.6 0.0 copy-done.8
  28.6 69.9 %all-to-all-done = bf16[2,128,96,128]{3,2,0,1:T(8,128)(2,1)} async-done(((bf16[2,128,96,128]{3,2,0,1:T(8,128)(2,1)}), bf16[2,128,96,128]{3,2,0,1:T(8,128)(2,1)}, u32[]{:S(2)}, u32[]{:S(2)}) %all-to-all-start) | async-done | bytes 6291488 | tf_op jit(solution)/shard_map/all_to_all | solution.py:31
  98.4 7.4 %copy.50 = bf16[2,32,4,96,128]{4,3,2,1,0:T(8,128)(2,1)} copy(bf16[2,32,4,96,128]{4,3,0,1,2:T(8,128)(2,1)} %bitcast.2) | data formatting | bytes 12582912 | tf_op jit(solution)/shard_map/all_to_all | solution.py:31
  105.8 9.0 %copy.51 = bf16[2,32,384,128]{2,1,0,3:T(8,128)(2,1)} copy(bf16[2,32,384,128]{3,2,1,0:T(8,128)(2,1)} %bitcast.54) | data formatting | bytes 12582912 | tf_op jit(solution)/shard_map/all_to_all | solution.py:31
  114.9 3.4 gather_fusion
  118.3 0.8 select_bitcast_fusion
  119.0 0.0 all-gather.2.cloned.1.call-update
  119.1 0.1 copy.56
  119.2 0.6 gather_fusion.1
  119.8 0.1 bitcast_select_fusion
  119.9 159.3 %all_gather.7 = bf16[1,1,384,256]{2,1,0,3:T(2,128)(2,1)S(1)} all-gather(bf16[1,1,384,4]{2,1,0,3:T(2,128)(2,1)S(1)} %copy.57), channel_id=1, replica_groups=mesh['freq'=4,'rcv'=64] {'rcv'}, dimensions={3}, use_global_device_ids=true | all-gather | bytes 199680 | tf_op jit(solution)/shard_map/all_gather | solution.py:38
  279.2 0.4 copy.58
  279.6 0.2 fusion.7
  279.8 4.0 copy.49
  283.8 1.4 fusion.28
  285.2 0.4 copy.53
  285.6 0.0 copy-start.3
  285.6 2.3 copy.55
  287.9 12.9 %all-gather.2.cloned.1.call-done = bf16[2,32,384,256]{2,1,0,3:T(8,128)(2,1)} async-done(((bf16[2,32,384,4]{2,1,0,3:T(8,128)(2,1)}), bf16[2,32,384,256]{2,1,0,3:T(8,128)(2,1)}) %all-gather.2.cloned.1.call-update) | async-done | bytes 12582928 | tf_op jit(solution)/shard_map/all_gather | solution.py:37
  300.8 6.3 %fusion.27 = (bf16[1,32,384,256]{2,1,0,3:T(8,128)(2,1)S(1)}, bf16[1,32,384,256]{2,1,0,3:T(8,128)(2,1)S(1)}) fusion(bf16[2,32,384,256]{2,1,0,3:T(8,128)(2,1)} %all-gather.2.cloned.1.call-done), kind=kLoop, calls=%fused_computation.52 | loop fusion | bytes 25165824 | tf_op jit(solution)/shard_map/slice | solution.py:43
  307.2 0.0 copy-start.2
  307.2 0.0 copy-start.1
  307.2 0.0 copy-done.3
  307.2 0.0 copy-start.5
  307.2 4.3 %fusion.3 = f32[32,256,128]{2,1,0:T(8,128)S(1)} fusion(bf16[32,384,128]{2,1,0:T(8,128)(2,1)S(1)} %bitcast.57, bf16[1,32,384,256]{2,1,0,3:T(8,128)(2,1)S(1)} %get-tuple-element.17), kind=kOutput, calls=%fused_computation.11 | convolution fusion | flops 805306368 | bytes 13631488 | tf_op jit(solution)/shard_map/fws,fwc->fsc/dot_general | solution.py:39
  311.5 0.0 copy-done.2
  311.5 0.8 copy-done.1
  312.3 0.0 copy-done.5
  312.3 4.5 %divide_convert_fusion.1 = bf16[32,256,128]{2,1,0:T(8,128)(2,1)S(1)} fusion(f32[32,256,128]{2,1,0:T(8,128)S(1)} %fusion.3, f32[256,128]{1,0:T(8,128)S(1)} %fusion.7, bf16[32,384,128]{2,1,0:T(8,128)(2,1)S(1)} %bitcast.60, bf16[1,32,384,256]{2,1,0,3:T(8,128)(2,1)S(1)} %get-tuple-element.16), kind=kOutput, calls=%fused_computation.19 | convolution fusion | flops 808452096 | bytes 15859712 | tf_op jit(solution)/shard_map/fws,fwc->fsc/dot_general | solution.py:42
  316.8 2.7 copy.59
  319.5 19.4 %all-to-all-start.1 = ((bf16[32,256,128]{2,0,1:T(8,128)(2,1)}), bf16[32,256,128]{2,0,1:T(8,128)(2,1)S(1)}, u32[]{:S(2)}, u32[]{:S(2)}) async-start(bf16[32,256,128]{2,0,1:T(8,128)(2,1)} %copy.59), calls=%async_computation.1 | async-start | bytes 4194304 | tf_op jit(solution)/shard_map/all_to_all | solution.py:58
  338.9 0.0 copy-start.4
  338.9 7.9 %fusion.2 = f32[32,256,128]{2,1,0:T(8,128)S(1)} fusion(bf16[32,384,128]{2,1,0:T(8,128)(2,1)} %bitcast.59, bf16[1,32,384,256]{2,1,0,3:T(8,128)(2,1)} %copy-done.2), kind=kOutput, calls=%fused_computation.10 | convolution fusion | flops 805306368 | bytes 13631488 | tf_op jit(solution)/shard_map/fws,fwc->fsc/dot_general | solution.py:45
  346.8 0.0 copy-done.4
  346.8 7.6 %divide_convert_fusion = bf16[32,256,128]{2,1,0:T(8,128)(2,1)S(1)} fusion(f32[32,256,128]{2,1,0:T(8,128)S(1)} %fusion.2, f32[256,128]{1,0:T(8,128)S(1)} %fusion.7, bf16[32,384,128]{2,1,0:T(8,128)(2,1)S(1)} %bitcast.58, bf16[1,32,384,256]{2,1,0,3:T(8,128)(2,1)} %copy-done.1), kind=kOutput, calls=%fused_computation.18 | convolution fusion | flops 808452096 | bytes 15859712 | tf_op jit(solution)/shard_map/fws,fwc->fsc/dot_general | solution.py:48
  354.4 0.0 copy-start.7
  354.4 2.7 copy.61
  357.1 6.6 %all-to-all-done.1 = bf16[32,256,128]{2,0,1:T(8,128)(2,1)S(1)} async-done(((bf16[32,256,128]{2,0,1:T(8,128)(2,1)}), bf16[32,256,128]{2,0,1:T(8,128)(2,1)S(1)}, u32[]{:S(2)}, u32[]{:S(2)}) %all-to-all-start.1) | async-done | bytes 2097184 | tf_op jit(solution)/shard_map/all_to_all | solution.py:58
  363.7 5.3 %all-to-all-start.2 = ((bf16[32,256,128]{2,0,1:T(8,128)(2,1)}), bf16[32,256,128]{2,0,1:T(8,128)(2,1)}, u32[]{:S(2)}, u32[]{:S(2)}) async-start(bf16[32,256,128]{2,0,1:T(8,128)(2,1)} %copy.61), calls=%async_computation.2 | async-start | bytes 4194304 | tf_op jit(solution)/shard_map/all_to_all | solution.py:59
  369.0 0.0 copy-done.7
  369.0 0.1 fusion.29
  369.1 2.0 copy.60
  371.0 0.0 copy-start
  371.0 22.9 %all-to-all-done.2 = bf16[32,256,128]{2,0,1:T(8,128)(2,1)} async-done(((bf16[32,256,128]{2,0,1:T(8,128)(2,1)}), bf16[32,256,128]{2,0,1:T(8,128)(2,1)}, u32[]{:S(2)}, u32[]{:S(2)}) %all-to-all-start.2) | async-done | bytes 2097184 | tf_op jit(solution)/shard_map/all_to_all | solution.py:59
  393.9 2.2 copy.62
  396.1 0.0 copy-done
  396.1 1.0 fusion.13
  397.1 2.5 select_reduce_fusion
  399.6 2.9 copy.63
  (6 shorter events, 0.1 us)
Async XLA Ops:
  11.7 1.0 copy-start.6
  20.0 8.6 %copy-start.8 = (s32[4]{0:T(128)S(1)}, s32[4]{0:T(128)}, u32[]{:S(2)}) copy-start(s32[4]{0:T(128)} %param.6) | copy-start | bytes 52
  20.0 78.5 %all-to-all-start = ((bf16[2,128,96,128]{3,2,0,1:T(8,128)(2,1)}), bf16[2,128,96,128]{3,2,0,1:T(8,128)(2,1)}, u32[]{:S(2)}, u32[]{:S(2)}) async-start(bf16[2,128,96,128]{3,2,0,1:T(8,128)(2,1)} %multiply_convert_fusion), calls=%async_computation | async-start | bytes 12582912 | tf_op jit(solution)/shard_map/all_to_all | solution.py:31
  28.6 272.3 %all-gather.2.cloned.1.call-start = ((), (), s32[]{:S(2)}) async-start(), calls=%async_computation.3 | async-start | bytes 12779520 | tf_op jit(solution)/shard_map/all_gather | solution.py:37
  285.6 21.6 %copy-start.3 = (bf16[1,32,4,96,128]{4,3,2,1,0:T(8,128)(2,1)}, bf16[1,32,4,96,128]{4,3,2,1,0:T(8,128)(2,1)S(1)}, u32[]{:S(2)}) copy-start(bf16[1,32,4,96,128]{4,3,2,1,0:T(8,128)(2,1)S(1)} %copy.53) | copy-start | bytes 9437188
  307.2 4.4 %copy-start.2 = (bf16[1,32,384,256]{2,1,0,3:T(8,128)(2,1)}, bf16[1,32,384,256]{2,1,0,3:T(8,128)(2,1)S(1)}, u32[]{:S(2)}) copy-start(bf16[1,32,384,256]{2,1,0,3:T(8,128)(2,1)S(1)} %get-tuple-element.17) | copy-start | bytes 18874372
  307.2 5.1 %copy-start.1 = (bf16[1,32,384,256]{2,1,0,3:T(8,128)(2,1)}, bf16[1,32,384,256]{2,1,0,3:T(8,128)(2,1)S(1)}, u32[]{:S(2)}) copy-start(bf16[1,32,384,256]{2,1,0,3:T(8,128)(2,1)S(1)} %get-tuple-element.16) | copy-start | bytes 18874372
  307.2 5.1 %copy-start.5 = (bf16[1,32,4,96,128]{4,3,2,1,0:T(8,128)(2,1)S(1)}, bf16[1,32,4,96,128]{4,3,2,1,0:T(8,128)(2,1)}, u32[]{:S(2)}) copy-start(bf16[1,32,4,96,128]{4,3,2,1,0:T(8,128)(2,1)} %copy.55) | copy-start | bytes 9437188
  319.5 44.2 %all-to-all-start.1 = ((bf16[32,256,128]{2,0,1:T(8,128)(2,1)}), bf16[32,256,128]{2,0,1:T(8,128)(2,1)S(1)}, u32[]{:S(2)}, u32[]{:S(2)}) async-start(bf16[32,256,128]{2,0,1:T(8,128)(2,1)} %copy.59), calls=%async_computation.1 | async-start | bytes 4194304 | tf_op jit(solution)/shard_map/all_to_all | solution.py:58
  338.9 7.9 %copy-start.4 = (bf16[1,32,4,96,128]{4,3,2,1,0:T(8,128)(2,1)S(1)}, bf16[1,32,4,96,128]{4,3,2,1,0:T(8,128)(2,1)}, u32[]{:S(2)}) copy-start(bf16[1,32,4,96,128]{4,3,2,1,0:T(8,128)(2,1)} %copy-done.3) | copy-start | bytes 9437188
  354.4 14.6 %copy-start.7 = (s32[64,128,2]{1,2,0:T(2,128)S(1)}, s32[64,128,2]{1,2,0:T(2,128)}, u32[]{:S(2)}) copy-start(s32[64,128,2]{1,2,0:T(2,128)} %param.7) | copy-start | bytes 196612
  363.7 30.2 %all-to-all-start.2 = ((bf16[32,256,128]{2,0,1:T(8,128)(2,1)}), bf16[32,256,128]{2,0,1:T(8,128)(2,1)}, u32[]{:S(2)}, u32[]{:S(2)}) async-start(bf16[32,256,128]{2,0,1:T(8,128)(2,1)} %copy.61), calls=%async_computation.2 | async-start | bytes 4194304 | tf_op jit(solution)/shard_map/all_to_all | solution.py:59
  371.0 25.1 %copy-start = (bf16[32,4,64,128]{3,0,1,2:T(8,128)(2,1)S(1)}, bf16[32,4,64,128]{3,0,1,2:T(8,128)(2,1)}, u32[]{:S(2)}) copy-start(bf16[32,4,64,128]{3,0,1,2:T(8,128)(2,1)} %copy.60) | copy-start | bytes 6291460
Sparse Core Ops, SparseCore 0:
  119.2 181.6 all-gather.1
where the time goes:
time: 410 us; the launch traced here: 409 us
  blocking collectives  159 us (39%)
  waiting for transfers between devices  112 us (27%)
  local copies, waits for them, and re-layouts  48.6 us (12%)
  starting transfers between devices  33.3 us (8%)
  matrix products  28 us (7%)
  between operations  14.3 us (3%)
  other arithmetic  13.6 us (3%)
    all_gather x1, blocking collectives, local(): source_valid = lax.all_gather(picked_valid, 'rcv', axis=3, tiled=True)  159 us
    all_to_all x1, waiting for transfers between devices, local(): lax.all_to_all(whitened, 'freq', split_axis=1, concat_axis=2, tiled=True)  69.9 us
    all_to_all x1, waiting for transfers between devices, local(): lax.all_to_all(stack_im, 'freq', split_axis=1, concat_axis=0, tiled=True)  22.9 us
    all_to_all x3, local copies, waits for them, and re-layouts, local(): lax.all_to_all(whitened, 'freq', split_axis=1, concat_axis=2, tiled=True)  20.4 us
    all_to_all x1, starting transfers between devices, local(): lax.all_to_all(stack_re, 'freq', split_axis=1, concat_axis=0, tiled=True)  19.4 us
    all_gather x1, waiting for transfers between devices, local(): source_part = lax.all_gather(picked, 'rcv', axis=3, tiled=True)  12.9 us
    all_to_all x1, starting transfers between devices, local(): lax.all_to_all(whitened, 'freq', split_axis=1, concat_axis=2, tiled=True)  8.59 us
  transfers between devices with their start and end apart: 4, of which 4 were waited for; matrix products, arithmetic and copies ran while one was open for 7% of the time, Pallas kernels for 0%

commit v1 on v0

--- a/solution.py
+++ b/solution.py
@@ -34,7 +34,15 @@
     picked = jnp.take(regrouped, offsets, axis=3)
     valid_half = valid.astype(jnp.bfloat16)
     picked_valid = jnp.take(valid_half, offsets, axis=1)[None, None]
-    source_part = lax.all_gather(picked, "rcv", axis=3, tiled=True)
+    source_part = jnp.concatenate(
+        lax.all_to_all(
+            jnp.stack([picked] * lax.axis_size("rcv"), 0),
+            split_axis=0,
+            concat_axis=0,
+            axis_name="rcv",
+        ),
+        3,
+    )
     source_valid = lax.all_gather(picked_valid, "rcv", axis=3, tiled=True)
     part_re = jnp.einsum(
         "fws,fwc->fsc", source_part[0], regrouped[0], preferred_element_type=jnp.float32

time: 410 us -> 719 us (1.75)
  blocking collectives: 159 us -> 421 us
  local copies, waits for them, and re-layouts: 48.6 us -> 99.8 us
  starting transfers between devices: 33.3 us -> 59.1 us
  between operations: 14.3 us -> 0.82 us
  waiting for transfers between devices: 112 us -> 103 us
  matrix products: 28 us -> 20.4 us
    all_gather x1, blocking collectives: 159 us -> 421 us  [local(): source_valid = lax.all_gather(picked_valid, 'rcv', axis=3, tiled=True)]
    squeeze x0 -> x2, local copies, waits for them, and re-layouts: none -> 21.6 us  [the longest x1 10.9 us: local(): source_part[1]]
    all_to_all x1, starting transfers between devices: 19.4 us -> 33.3 us  [local(): lax.all_to_all(stack_re, 'freq', split_axis=1, concat_axis=0, tiled=True)]
    slice x1 -> x2, local copies, waits for them, and re-layouts: 6.33 us -> 20 us  [local(): source_part[1]]
    all_gather x1 -> x0, waiting for transfers between devices: 12.9 us -> none  [local(): source_part = lax.all_gather(picked, 'rcv', axis=3, tiled=True)]
    all_to_all x0 -> x1, starting transfers between devices: none -> 12.8 us  [local(): lax.all_to_all(jnp.stack([picked] * lax.axis_size('rcv'), 0), split_axis=...]
    another operation x0 -> x1, local copies, waits for them, and re-layouts: none -> 7.32 us  [local(): jnp.stack([picked] * lax.axis_size('rcv'), 0)]
  transfers between devices with their start and end apart: 4 -> 4, of which waited for: 4 -> 3; matrix products, arithmetic and copies ran while one was open for 7% -> 4% of each run, Pallas kernels for 0% -> 0%
where the time goes in v1:
time: 719 us; the launch traced here: 717 us
  blocking collectives  421 us (59%)
  waiting for transfers between devices  103 us (14%)
  local copies, waits for them, and re-layouts  99.8 us (14%)
  starting transfers between devices  59.1 us (8%)
  matrix products  20.4 us (3%)
  other arithmetic  13 us (2%)
    all_gather x1, blocking collectives, local(): source_valid = lax.all_gather(picked_valid, 'rcv', axis=3, tiled=True)  421 us
    all_to_all x1, waiting for transfers between devices, local(): lax.all_to_all(whitened, 'freq', split_axis=1, concat_axis=2, tiled=True)  69.9 us
    all_to_all x1, starting transfers between devices, local(): lax.all_to_all(stack_re, 'freq', split_axis=1, concat_axis=0, tiled=True)  33.3 us
    all_to_all x1, waiting for transfers between devices, local(): lax.all_to_all(stack_im, 'freq', split_axis=1, concat_axis=0, tiled=True)  21.2 us
    all_to_all x3, local copies, waits for them, and re-layouts, local(): lax.all_to_all(whitened, 'freq', split_axis=1, concat_axis=2, tiled=True)  20.4 us
    slice x2, local copies, waits for them, and re-layouts, local(): source_part[1]  20 us
  transfers between devices with their start and end apart: 4, of which 3 were waited for; matrix products, arithmetic and copies ran while one was open for 4% of the time, Pallas kernels for 0%

profile of v1, /device:TPU:1, one launch (start us, length us, event | category | flops | bytes accessed | tf_op | source)
XLA Modules:
  0.0 717.2 jit_solution(11337690449416650101)
XLA Ops:
  0.6 4.6 copy_convert_fusion
  5.2 0.0 copy-start.4
  5.2 0.9 fusion.1
  6.2 0.0 copy-done.4
  6.2 7.2 %multiply_convert_fusion = bf16[2,128,96,128]{3,2,0,1:T(8,128)(2,1)} fusion(f32[96,128]{1,0:T(8,128)S(1)} %rsqrt_multiply_fusion, bf16[2,128,96,128]{3,2,1,0:T(8,128)(2,1)} %param.4), kind=kLoop, calls=%fused_computation.2 | loop fusion | flops 9437184 | bytes 12632064 | tf_op jit(solution)/shard_map/convert_element_type | solution.py:30
  13.4 0.0 copy-start.6
  13.4 8.6 %all-to-all-start = ((bf16[2,128,96,128]{3,2,0,1:T(8,128)(2,1)}), bf16[2,128,96,128]{3,2,0,1:T(8,128)(2,1)}, u32[]{:S(2)}, u32[]{:S(2)}) async-start(bf16[2,128,96,128]{3,2,0,1:T(8,128)(2,1)} %multiply_convert_fusion), calls=%async_computation | async-start | bytes 12582912 | tf_op jit(solution)/shard_map/all_to_all | solution.py:31
  22.1 0.0 copy-done.6
  22.1 69.9 %all-to-all-done = bf16[2,128,96,128]{3,2,0,1:T(8,128)(2,1)} async-done(((bf16[2,128,96,128]{3,2,0,1:T(8,128)(2,1)}), bf16[2,128,96,128]{3,2,0,1:T(8,128)(2,1)}, u32[]{:S(2)}, u32[]{:S(2)}) %all-to-all-start) | async-done | bytes 6291488 | tf_op jit(solution)/shard_map/all_to_all | solution.py:31
  91.9 7.4 %copy.52 = bf16[2,32,4,96,128]{4,3,2,1,0:T(8,128)(2,1)} copy(bf16[2,32,4,96,128]{4,3,0,1,2:T(8,128)(2,1)} %bitcast.2) | data formatting | bytes 12582912 | tf_op jit(solution)/shard_map/all_to_all | solution.py:31
  99.3 9.1 %copy.53 = bf16[2,32,384,128]{2,1,0,3:T(8,128)(2,1)} copy(bf16[2,32,384,128]{3,2,1,0:T(8,128)(2,1)} %bitcast.51) | data formatting | bytes 12582912 | tf_op jit(solution)/shard_map/all_to_all | solution.py:31
  108.4 3.4 gather_fusion
  111.8 0.1 select_bitcast_fusion
  111.9 0.2 copy.54
  112.0 7.3 %stack.2 = bf16[64,2,32,384,4]{3,4,2,1,0:T(4,128)(2,1)} broadcast(bf16[2,32,384,4]{2,3,1,0:T(4,128)(2,1)S(1)} %copy.54), dimensions={1,2,3,4} | broadcast | bytes 12779520 | tf_op jit(solution)/shard_map/stack | solution.py:39
  119.3 12.8 %all-to-all-start.1 = ((bf16[64,2,32,384,4]{3,4,2,1,0:T(4,128)(2,1)}), bf16[64,2,32,384,4]{3,4,2,1,0:T(4,128)(2,1)}, u32[]{:S(2)}, u32[]{:S(2)}) async-start(bf16[64,2,32,384,4]{3,4,2,1,0:T(4,128)(2,1)} %stack.2), calls=%async_computation.1 | async-start | bytes 25165824 | tf_op jit(solution)/shard_map/all_to_all | solution.py:38
  132.1 0.1 copy.59
  132.3 0.6 gather_fusion.1
  132.9 0.1 bitcast_select_fusion
  132.9 420.9 %all_gather.3 = bf16[1,1,384,256]{2,1,0,3:T(2,128)(2,1)S(1)} all-gather(bf16[1,1,384,4]{2,1,0,3:T(2,128)(2,1)S(1)} %copy.60), channel_id=1, replica_groups=mesh['freq'=4,'rcv'=64] {'rcv'}, dimensions={3}, use_global_device_ids=true | all-gather | bytes 199680 | tf_op jit(solution)/shard_map/all_gather | solution.py:46
  553.9 0.4 copy.61
  554.3 0.2 fusion.3
  554.5 3.9 copy.51
  558.5 1.4 fusion.24
  559.9 2.1 copy.56
  562.0 2.1 copy.58
  564.1 0.0 all-to-all-done.1
  564.1 11.3 %fusion.23 = (bf16[1,32,384,64,4]{2,4,1,0,3:T(4,128)(2,1)}, bf16[1,32,384,64,4]{2,4,1,0,3:T(4,128)(2,1)S(1)}) fusion(bf16[2,32,384,64,4]{2,4,1,0,3:T(4,128)(2,1)} %bitcast.5), kind=kLoop, calls=%fused_computation.46 | loop fusion | bytes 25165824 | tf_op jit(solution)/shard_map/slice | solution.py:51
  575.5 6.0 copy.55
  581.4 10.7 %squeeze.10 = bf16[32,384,256]{1,2,0:T(8,128)(2,1)} reshape(bf16[1,32,384,64,4]{2,4,3,1,0:T(4,128)(2,1)} %copy.55) | data formatting | bytes 12582912 | tf_op jit(solution)/shard_map/squeeze | solution.py:48
  592.2 8.6 %copy.57 = bf16[1,32,384,64,4]{2,4,3,1,0:T(4,128)(2,1)} copy(bf16[1,32,384,64,4]{2,4,1,0,3:T(4,128)(2,1)} %get-tuple-element.16) | data formatting | bytes 12582912 | tf_op jit(solution)/shard_map/slice | solution.py:51
  600.8 0.0 copy-start
  600.8 10.9 %squeeze.12 = bf16[32,384,256]{1,2,0:T(8,128)(2,1)} reshape(bf16[1,32,384,64,4]{2,4,3,1,0:T(4,128)(2,1)} %copy.57) | data formatting | bytes 12582912 | tf_op jit(solution)/shard_map/squeeze | solution.py:51
  611.7 0.0 copy-done
  611.7 0.0 copy-start.1
  611.7 0.0 copy-start.3
  611.7 4.7 fusion.26
  616.4 0.0 copy-done.1
  616.4 0.8 copy-done.3
  617.2 1.8 divide_convert_fusion.1
  619.0 2.7 copy.62
  621.7 33.3 %all-to-all-start.2 = ((bf16[32,256,128]{2,0,1:T(8,128)(2,1)}), bf16[32,256,128]{2,0,1:T(8,128)(2,1)}, u32[]{:S(2)}, u32[]{:S(2)}) async-start(bf16[32,256,128]{2,0,1:T(8,128)(2,1)} %copy.62), calls=%async_computation.2 | async-start | bytes 4194304 | tf_op jit(solution)/shard_map/all_to_all | solution.py:66
  655.0 5.5 fusion.27
  660.5 4.6 divide_convert_fusion
  665.1 0.0 copy-start.5
  665.1 2.7 copy.64
  667.8 12.2 %all-to-all-done.2 = bf16[32,256,128]{2,0,1:T(8,128)(2,1)} async-done(((bf16[32,256,128]{2,0,1:T(8,128)(2,1)}), bf16[32,256,128]{2,0,1:T(8,128)(2,1)}, u32[]{:S(2)}, u32[]{:S(2)}) %all-to-all-start.2) | async-done | bytes 2097184 | tf_op jit(solution)/shard_map/all_to_all | solution.py:66
  679.9 4.4 all-to-all-start.3
  684.4 0.0 copy-done.5
  684.4 0.1 fusion.25
  684.4 3.6 copy.63
  688.0 21.2 %all-to-all-done.3 = bf16[32,256,128]{2,0,1:T(8,128)(2,1)S(1)} async-done(((bf16[32,256,128]{2,0,1:T(8,128)(2,1)}), bf16[32,256,128]{2,0,1:T(8,128)(2,1)S(1)}, u32[]{:S(2)}, u32[]{:S(2)}) %all-to-all-start.3) | async-done | bytes 2097184 | tf_op jit(solution)/shard_map/all_to_all | solution.py:67
  709.2 0.0 copy-start.2
  709.2 0.6 copy.65
  709.8 0.9 copy-done.2
  710.8 1.0 fusion.9
  711.8 2.6 select_reduce_fusion
  714.3 2.9 copy.66
  (6 shorter events, 0.1 us)
Async XLA Ops:
  5.2 1.0 copy-start.4
  13.4 8.6 %copy-start.6 = (s32[4]{0:T(128)S(1)}, s32[4]{0:T(128)}, u32[]{:S(2)}) copy-start(s32[4]{0:T(128)} %param.6) | copy-start | bytes 52
  13.4 78.5 %all-to-all-start = ((bf16[2,128,96,128]{3,2,0,1:T(8,128)(2,1)}), bf16[2,128,96,128]{3,2,0,1:T(8,128)(2,1)}, u32[]{:S(2)}, u32[]{:S(2)}) async-start(bf16[2,128,96,128]{3,2,0,1:T(8,128)(2,1)} %multiply_convert_fusion), calls=%async_computation | async-start | bytes 12582912 | tf_op jit(solution)/shard_map/all_to_all | solution.py:31
  119.3 444.8 %all-to-all-start.1 = ((bf16[64,2,32,384,4]{3,4,2,1,0:T(4,128)(2,1)}), bf16[64,2,32,384,4]{3,4,2,1,0:T(4,128)(2,1)}, u32[]{:S(2)}, u32[]{:S(2)}) async-start(bf16[64,2,32,384,4]{3,4,2,1,0:T(4,128)(2,1)} %stack.2), calls=%async_computation.1 | async-start | bytes 25165824 | tf_op jit(solution)/shard_map/all_to_all | solution.py:38
  600.8 10.9 %copy-start = (bf16[1,32,4,96,128]{4,3,2,1,0:T(8,128)(2,1)S(1)}, bf16[1,32,4,96,128]{4,3,2,1,0:T(8,128)(2,1)}, u32[]{:S(2)}) copy-start(bf16[1,32,4,96,128]{4,3,2,1,0:T(8,128)(2,1)} %copy.56) | copy-start | bytes 9437188
  611.7 4.7 copy-start.1
  611.7 5.6 copy-start.3
  621.7 58.2 %all-to-all-start.2 = ((bf16[32,256,128]{2,0,1:T(8,128)(2,1)}), bf16[32,256,128]{2,0,1:T(8,128)(2,1)}, u32[]{:S(2)}, u32[]{:S(2)}) async-start(bf16[32,256,128]{2,0,1:T(8,128)(2,1)} %copy.62), calls=%async_computation.2 | async-start | bytes 4194304 | tf_op jit(solution)/shard_map/all_to_all | solution.py:66
  665.1 19.3 %copy-start.5 = (s32[64,128,2]{1,2,0:T(2,128)S(1)}, s32[64,128,2]{1,2,0:T(2,128)}, u32[]{:S(2)}) copy-start(s32[64,128,2]{1,2,0:T(2,128)} %param.7) | copy-start | bytes 196612
  679.9 29.3 %all-to-all-start.3 = ((bf16[32,256,128]{2,0,1:T(8,128)(2,1)}), bf16[32,256,128]{2,0,1:T(8,128)(2,1)S(1)}, u32[]{:S(2)}, u32[]{:S(2)}) async-start(bf16[32,256,128]{2,0,1:T(8,128)(2,1)} %copy.64), calls=%async_computation.3 | async-start | bytes 4194304 | tf_op jit(solution)/shard_map/all_to_all | solution.py:67
  709.2 1.6 copy-start.2
